TPU v7x, 1024 devices: a whole 4x4x32 slice. The times are simulated.
1024 devices in a mesh: section: 16 (over y, x), expert: 64 (over z, core).
Axes of the slice: x: 4, y: 4, z: 32, core: 2. Of those that a mesh axis runs over, the one named last changes fastest.
Arguments:
- cotangent: bfloat16 [131072, 4096], P(('section', 'expert')), may hold values from -6 to 6
- expert_ids: int32 [131072, 1], P(('section', 'expert')), may hold values from 0 to 63; in each aligned block of 128 rows (0 to 127, 128 to 255, ...) at most 4 rows name the same one
- route_weight: float32 [131072], P(('section', 'expert')), may hold values from 0.1 to 1
- saved_preact: bfloat16 [131072, 2048], P(('section', 'expert')), may hold values from -6 to 6
- down_weight: bfloat16 [64, 1024, 4096], P('expert'), may hold values from -0.09375 to 0.09375
Outputs:
- d_preact: bfloat16 [131072, 2048], P(('section', 'expert'))
- d_route: float32 [131072], P(('section', 'expert'))
Inputs may be any that keep to these rules, and one draw needn't show every extreme that they name: `expert_ids`: at most 4 of the 128 tokens of one device name the same expert, and on some devices one expert is named by exactly 4 of them.
All inputs are finite; a program needn't handle non-finite values.
Results may differ from a plain program's by a relative error of at most 0.0049.
Values may be sent and summed in bfloat16 or wider, within the bound.
No kernel may reach another device: no remote copies, remote signals or barrier semaphores. Data moves between devices by JAX's collectives and lax.ppermute only.
A program may use at most 32 MiB of HBM per device.

v0:
```python
import jax
import jax.numpy as jnp
from jax import lax
from jax.sharding import PartitionSpec as P


def shifted(block, axis, distance):
    devices = range(lax.axis_size(axis))
    route = [((i - distance) % len(devices), i) for i in devices]
    return lax.ppermute(block, axis, route)


def expert_products(received, weight):
    dims = (((1,), (1,)), ((), ()))
    return lax.dot_general(received, weight, dims, preferred_element_type=jnp.float32).astype(
        jnp.bfloat16
    )


def dispatch_rows(row_data, route_index, weight):
    token_count = row_data.shape[0]
    experts = lax.axis_size("expert")
    slot_cap = max(2, 2 * token_count // experts)
    onehot = (route_index[:, None] == jnp.arange(experts, dtype=jnp.int32)[None, :]).astype(
        jnp.int32
    )
    slot_rank = jnp.sum((jnp.cumsum(onehot, axis=0) - 1) * onehot, axis=1)
    flat_slot = route_index * slot_cap + slot_rank
    send_buffer = (
        jnp.zeros((experts * slot_cap, row_data.shape[1]), row_data.dtype)
        .at[flat_slot]
        .set(row_data)
    )
    received = lax.all_to_all(send_buffer, "expert", split_axis=0, concat_axis=0, tiled=True)
    products = expert_products(received, weight)
    back_rows = lax.all_to_all(products, "expert", split_axis=0, concat_axis=0, tiled=True)
    return back_rows[flat_slot]


def local(cotangent, expert_ids, route_weight, saved_preact, down_weight):
    route_index = expert_ids[:, 0]
    weight = down_weight[0]
    incoming = shifted(cotangent, "section", -1)
    back_hidden = dispatch_rows(incoming, route_index, weight)
    width = weight.shape[0]
    gate_value = saved_preact[:, :width].astype(jnp.float32)
    up_value = saved_preact[:, width:].astype(jnp.float32)
    sigmoid_gate = jax.nn.sigmoid(gate_value)
    activated = gate_value * sigmoid_gate
    hidden = activated * up_value
    result_float = back_hidden.astype(jnp.float32)
    d_route = jnp.sum(result_float * hidden, axis=1)
    grad_hidden = route_weight[:, None] * result_float
    d_gate = grad_hidden * up_value * sigmoid_gate * (1.0 + gate_value * (1.0 - sigmoid_gate))
    d_up = grad_hidden * activated
    d_preact = jnp.concatenate([d_gate, d_up], axis=1).astype(jnp.bfloat16)
    return (d_preact, d_route)


def solution(mesh):
    in_specs = (
        P(("section", "expert"), None),
        P(("section", "expert"), None),
        P(("section", "expert")),
        P(("section", "expert"), None),
        P("expert", None, None),
    )
    out_specs = (P(("section", "expert"), None), P(("section", "expert")))
    return jax.shard_map(local, mesh=mesh, in_specs=in_specs, out_specs=out_specs, check_vma=False)
```

profile of v0, /device:TPU:30, one launch (start us, length us, event | category | flops | bytes accessed | tf_op | source)
XLA Modules:
  0.0 348.6 jit_solution(11328744773707404574)
XLA Ops:
  0.6 2.7 collective-permute-start
  3.4 0.7 fusion.17
  4.1 0.2 reduce_window_sum.11
  4.3 0.8 select_reduce_fusion
  5.1 0.7 fusion.18
  5.8 25.2 %collective-permute-done = bf16[128,4096]{1,0:T(8,128)(2,1)S(1)} collective-permute-done((bf16[128,4096]{1,0:T(8,128)(2,1)}, bf16[128,4096]{1,0:T(8,128)(2,1)S(1)}, u32[]{:S(2)}, u32[]{:S(2)}) %collective-permute-start) | collective-permute-done | bytes 1048608 | tf_op jit(solution)/shard_map/ppermute | solution.py:10
  31.0 2.7 scatter_custom_fusion
  33.7 2.2 all_to_all.16
  35.9 229.9 %all_to_all.24 = bf16[64,4,4096]{2,1,0:T(4,128)(2,1)S(1)} all-to-all(bf16[64,4,4096]{2,1,0:T(4,128)(2,1)} %all_to_all.16), channel_id=1, replica_groups=mesh['section'=16,'expert'=64] {'expert'}, dimensions={0} | all-to-all | bytes 4194304 | tf_op jit(solution)/shard_map/all_to_all | solution.py:34
  265.8 2.1 all_to_all.18
  267.9 6.4 %fusion.2 = bf16[256,1024]{1,0:T(8,128)(2,1)S(1)} fusion(bf16[256,4096]{1,0:T(8,128)(2,1)} %all_to_all.18, bf16[1,1024,4096]{2,1,0:T(8,128)(2,1)} %param.9), kind=kOutput, calls=%fused_computation.4 | convolution fusion | flops 2147745792 | bytes 11010048 | tf_op jit(solution)/shard_map/dot_general | solution.py:15
  274.3 1.0 all_to_all.19
  275.3 0.0 copy-start
  275.3 0.0 copy-start.1
  275.3 4.8 %all-to-all-start.1 = ((bf16[64,4,1024]{2,1,0:T(4,128)(2,1)}), bf16[64,4,1024]{2,1,0:T(4,128)(2,1)S(1)}, u32[]{:S(2)}, u32[]{:S(2)}) async-start(bf16[64,4,1024]{2,1,0:T(4,128)(2,1)} %all_to_all.19), calls=%async_computation.1 | async-start | bytes 1048576 | tf_op jit(solution)/shard_map/all_to_all | solution.py:36
  280.0 65.7 %all-to-all-done.1 = bf16[64,4,1024]{2,1,0:T(4,128)(2,1)S(1)} async-done(((bf16[64,4,1024]{2,1,0:T(4,128)(2,1)}), bf16[64,4,1024]{2,1,0:T(4,128)(2,1)S(1)}, u32[]{:S(2)}, u32[]{:S(2)}) %all-to-all-start.1) | async-done | bytes 524320 | tf_op jit(solution)/shard_map/all_to_all | solution.py:36
  345.8 0.1 all_to_all.21
  345.9 0.9 gather_fusion
  346.8 0.0 copy-done
  346.8 0.0 copy-done.1
  346.8 1.0 fusion.12
  347.8 0.8 pad_maximum_fusion
  (1 shorter events, 0.0 us)
Async XLA Ops:
  0.6 30.3 %collective-permute-start = (bf16[128,4096]{1,0:T(8,128)(2,1)}, bf16[128,4096]{1,0:T(8,128)(2,1)S(1)}, u32[]{:S(2)}, u32[]{:S(2)}) collective-permute-start(bf16[128,4096]{1,0:T(8,128)(2,1)} %param.5), channel_id=1, source_target_pairs={{64,0},{128,64},{192,128},{256,192},{320,256},{384,320},{448,384},... | collective-permute-start | bytes 3145736 | tf_op jit(solution)/shard_map/ppermute | solution.py:10
  275.3 71.5 %copy-start = (bf16[128,2048]{1,0:T(8,128)(2,1)S(1)}, bf16[128,2048]{1,0:T(8,128)(2,1)}, u32[]{:S(2)}) copy-start(bf16[128,2048]{1,0:T(8,128)(2,1)} %param.8) | copy-start | bytes 1572868
  275.3 71.5 %copy-start.1 = (f32[128]{0:T(128)S(1)}, f32[128]{0:T(128)}, u32[]{:S(2)}) copy-start(f32[128]{0:T(128)} %param.7) | copy-start | bytes 1540
  275.3 70.5 %all-to-all-start.1 = ((bf16[64,4,1024]{2,1,0:T(4,128)(2,1)}), bf16[64,4,1024]{2,1,0:T(4,128)(2,1)S(1)}, u32[]{:S(2)}, u32[]{:S(2)}) async-start(bf16[64,4,1024]{2,1,0:T(4,128)(2,1)} %all_to_all.19), calls=%async_computation.1 | async-start | bytes 1048576 | tf_op jit(solution)/shard_map/all_to_all | solution.py:36
where the time goes:
time: 349 us
  blocking collectives  230 us (66%)
  waiting for transfers between devices  90.9 us (26%)
  local copies, waits for them, and re-layouts  9 us (3%)
  starting transfers between devices  7.5 us (2%)
  matrix products  6.38 us (2%)
  other arithmetic  4.22 us (1%)
    all_to_all x1, blocking collectives, dispatch_rows(): lax.all_to_all(send_buffer, 'expert', split_axis=0, concat_axis=0, tiled=...  230 us
    all_to_all x1, waiting for transfers between devices, dispatch_rows(): lax.all_to_all(products, 'expert', split_axis=0, concat_axis=0, tiled=True)  65.7 us
    ppermute x1, waiting for transfers between devices, shifted(): return lax.ppermute(block, axis, route)  25.2 us
  transfers between devices with their start and end apart: 2, of which 2 were waited for; matrix products, arithmetic and copies ran while one was open for 1% of the time, Pallas kernels for 0%

commit v1 on v0

v1 whole, which is shorter than its diff:
```python
import jax
import jax.numpy as jnp
from jax import lax
from jax.sharding import PartitionSpec as P

SLOTS = 2
ROUND = 16


def shifted(block, axis, distance):
    devices = range(lax.axis_size(axis))
    route = [((i - distance) % len(devices), i) for i in devices]
    return lax.ppermute(block, axis, route)


def expert_products(rows, weight):
    dims = (((1,), (1,)), ((), ()))
    return lax.dot_general(rows, weight, dims, preferred_element_type=jnp.float32).astype(
        jnp.bfloat16
    )


def onehot(left, right):
    return ((left[:, None] == right[None, :]) & (left[:, None] >= 0)).astype(jnp.bfloat16)


def pick(selection, rows):
    return jnp.dot(selection, rows, preferred_element_type=jnp.float32).astype(rows.dtype)


def count_before(flags):
    count = flags.shape[0]
    earlier = jnp.arange(count)[None, :] < jnp.arange(count)[:, None]
    return jnp.sum((flags[None, :] & earlier).astype(jnp.int32), axis=1)


def placed(expert):
    count = expert.shape[0]
    earlier = jnp.arange(count)[None, :] < jnp.arange(count)[:, None]
    same = expert[:, None] == expert[None, :]
    rank = jnp.sum((same & earlier).astype(jnp.int32), axis=1)
    beyond = rank >= SLOTS
    slot = jnp.where(beyond, -1, expert * SLOTS + rank)
    extra = jnp.where(beyond, count_before(beyond), -1)
    return slot, extra, jnp.sum(beyond.astype(jnp.int32))


def extra_round(turn, extra, expert, rows, weight):
    experts = lax.axis_size("expert")
    me = lax.axis_index("expert")
    turn_place = jnp.where(extra >= 0, extra - turn * ROUND, -1)
    selection = onehot(jnp.arange(ROUND, dtype=jnp.int32), turn_place)
    sent = pick(selection, rows)
    name = jnp.sum(selection * (expert + 1).astype(jnp.bfloat16)[None, :], axis=1, keepdims=True)
    sent = jnp.concatenate([sent, jnp.broadcast_to(name, (ROUND, 128))], axis=1)
    seen = lax.all_gather(sent, "expert", axis=0, tiled=True)
    width = rows.shape[1]
    mine = seen[:, width].astype(jnp.int32) == me + 1
    depth = experts * SLOTS
    order = jnp.where(mine, count_before(mine), -1)
    chosen = onehot(jnp.arange(depth, dtype=jnp.int32), order)
    products = expert_products(pick(chosen, seen[:, :width]), weight)
    spread = pick(onehot(order, jnp.arange(depth, dtype=jnp.int32)), products)
    back = lax.psum_scatter(spread, "expert", scatter_dimension=0, tiled=True)
    return pick(onehot(turn_place, jnp.arange(ROUND, dtype=jnp.int32)), back)


def local(cotangent, expert_ids, route_weight, saved_preact, down_weight):
    weight = down_weight[0]
    width = weight.shape[0]
    experts = lax.axis_size("expert")
    expert = shifted(expert_ids[:, 0], "section", 1)

    slot, extra, beyond = placed(expert)
    rounds = lax.pmax((beyond + ROUND - 1) // ROUND, ("section", "expert"))
    places = jnp.arange(experts * SLOTS, dtype=jnp.int32)

    first = extra_round(0, extra, expert, cotangent, weight)

    send = pick(onehot(places, slot), cotangent)
    received = lax.all_to_all(send, "expert", split_axis=0, concat_axis=0, tiled=True)
    products = expert_products(received, weight)
    returned = lax.all_to_all(products, "expert", split_axis=0, concat_axis=0, tiled=True)
    result = pick(onehot(slot, places), returned) + first

    def more(state):
        return state[0] < rounds

    def step(state):
        turn, total = state
        return turn + 1, total + extra_round(turn, extra, expert, cotangent, weight)

    result = lax.while_loop(more, step, (jnp.int32(1), result))[1]

    back_hidden = shifted(result, "section", -1)
    gate_value = saved_preact[:, :width].astype(jnp.float32)
    up_value = saved_preact[:, width:].astype(jnp.float32)
    sigmoid_gate = jax.nn.sigmoid(gate_value)
    activated = gate_value * sigmoid_gate
    hidden = activated * up_value
    result_float = back_hidden.astype(jnp.float32)
    d_route = jnp.sum(result_float * hidden, axis=1)
    grad_hidden = route_weight[:, None] * result_float
    d_gate = grad_hidden * up_value * sigmoid_gate * (1.0 + gate_value * (1.0 - sigmoid_gate))
    d_up = grad_hidden * activated
    d_preact = jnp.concatenate([d_gate, d_up], axis=1).astype(jnp.bfloat16)
    return (d_preact, d_route)


def solution(mesh):
    in_specs = (
        P(("section", "expert"), None),
        P(("section", "expert"), None),
        P(("section", "expert")),
        P(("section", "expert"), None),
        P("expert", None, None),
    )
    out_specs = (P(("section", "expert"), None), P(("section", "expert")))
    return jax.shard_map(local, mesh=mesh, in_specs=in_specs, out_specs=out_specs, check_vma=False)
```

time: 349 us -> 493 us (1.41)
  waiting for transfers between devices: 90.9 us -> 236 us
  blocking collectives: 230 us -> 156 us
  starting transfers between devices: 7.5 us -> 50.1 us
  matrix products: 6.38 us -> 23.5 us
  between operations: 0.71 us -> 14.9 us
    all_to_all x1 -> x0, blocking collectives: 230 us -> none  [dispatch_rows(): lax.all_to_all(send_buffer, 'expert', split_axis=0, concat_axis=0, tiled=...]
    all_gather x0 -> x1, waiting for transfers between devices: none -> 190 us  [extra_round(): seen = lax.all_gather(sent, 'expert', axis=0, tiled=True)]
    pmax x0 -> x1, blocking collectives: none -> 156 us  [local(): rounds = lax.pmax((beyond + ROUND - 1) // ROUND, ('section', 'expert'))]
    all_to_all x1 -> x2, waiting for transfers between devices: 65.7 us -> 0.01 us  [the longest x1 0.01 us: local(): lax.all_to_all(send, 'expert', split_axis=0, concat_axis=0, tiled=True)]
    reduce_scatter x0 -> x1, waiting for transfers between devices: none -> 35.7 us  [extra_round(): back = lax.psum_scatter(spread, 'expert', scatter_dimension=0, tiled=True)]
    all_to_all x1 -> x2, starting transfers between devices: 4.77 us -> 33.1 us  [the longest x1 19.1 us: local(): lax.all_to_all(send, 'expert', split_axis=0, concat_axis=0, tiled=True)]
    dot_general x1 -> x7, matrix products: 6.38 us -> 23.5 us  [the longest x6 17.2 us: pick(): jnp.dot(selection, rows, preferred_element_type=jnp.float32)]
    ppermute x1 -> x2, waiting for transfers between devices: 25.2 us -> 10.7 us  [shifted(): return lax.ppermute(block, axis, route)]
  transfers between devices with their start and end apart: 2 -> 6, of which waited for: 2 -> 4; matrix products, arithmetic and copies ran while one was open for 1% -> 5% of each run, Pallas kernels for 0% -> 0%
where the time goes in v1:
time: 493 us; the launch traced here: 492 us
  waiting for transfers between devices  236 us (48%)
  blocking collectives  156 us (32%)
  starting transfers between devices  50.1 us (10%)
  matrix products  23.5 us (5%)
  between operations  14.9 us (3%)
  other arithmetic  6.04 us (1%)
    all_gather x1, waiting for transfers between devices, extra_round(): seen = lax.all_gather(sent, 'expert', axis=0, tiled=True)  190 us
    pmax x1, blocking collectives, local(): rounds = lax.pmax((beyond + ROUND - 1) // ROUND, ('section', 'expert'))  156 us
    reduce_scatter x1, waiting for transfers between devices, extra_round(): back = lax.psum_scatter(spread, 'expert', scatter_dimension=0, tiled=True)  35.7 us
    all_to_all x1, starting transfers between devices, local(): lax.all_to_all(send, 'expert', split_axis=0, concat_axis=0, tiled=True)  19.1 us
    dot_general x6, matrix products, pick(): jnp.dot(selection, rows, preferred_element_type=jnp.float32)  17.2 us
    ppermute x2, starting transfers between devices, shifted(): return lax.ppermute(block, axis, route)  16.9 us
    all_to_all x1, starting transfers between devices, local(): lax.all_to_all(products, 'expert', split_axis=0, concat_axis=0, tiled=True)  14 us
    ppermute x2, waiting for transfers between devices, shifted(): return lax.ppermute(block, axis, route)  10.7 us
  transfers between devices with their start and end apart: 6, of which 4 were waited for; matrix products, arithmetic and copies ran while one was open for 5% of the time, Pallas kernels for 0%

profile of v1, /device:TPU:30, one launch (start us, length us, event | category | flops | bytes accessed | tf_op | source)
XLA Modules:
  0.0 492.4 jit_solution(382121244568837783)
XLA Ops:
  7.2 0.0 all-gather.3.cloned.1.call-start
  7.2 14.7 %collective-permute-start = (s32[128]{0:T(128)}, s32[128]{0:T(128)S(1)}, u32[]{:S(2)}, u32[]{:S(2)}) collective-permute-start(s32[128]{0:T(128)} %bitcast.32), channel_id=1, source_target_pairs={{960,0},{0,64},{64,128},{128,192},{192,256},{256,320},{320,384},{3... | collective-permute-start | bytes 1544 | tf_op jit(solution)/shard_map/ppermute | solution.py:13
  21.9 1.4 collective-permute-done
  23.3 0.2 convert_reduce_fusion.3
  23.5 0.1 convert_reduce_fusion.2
  23.6 0.1 fusion.53
  23.8 1.5 convolution_convert_fusion.5
  25.2 0.1 broadcast_in_dim.29
  25.3 0.7 pad_maximum_fusion.2
  26.0 0.0 all-gather.3.cloned.1.call-update
  26.0 1.7 convolution_convert_fusion.4
  27.7 1.5 all_to_all.16
  29.2 19.1 %all-to-all-start = ((bf16[64,2,4096]{2,1,0:T(2,128)(2,1)}), bf16[64,2,4096]{2,1,0:T(2,128)(2,1)}, u32[]{:S(2)}, u32[]{:S(2)}) async-start(bf16[64,2,4096]{2,1,0:T(2,128)(2,1)} %all_to_all.16), calls=%async_computation.1 | async-start | bytes 2097152 | tf_op jit(solution)/shard_map/all_to_all | solution.py:81
  48.3 0.0 reduce-scatter.3.cloned.1.call-start
  48.4 189.9 %all-gather.3.cloned.1.call-done = bf16[1024,4224]{1,0:T(8,128)(2,1)} async-done(((bf16[16,4224]{1,0:T(8,128)(2,1)}), bf16[1024,4224]{1,0:T(8,128)(2,1)}) %all-gather.3.cloned.1.call-update) | async-done | bytes 8650768 | tf_op jit(solution)/shard_map/all_gather | solution.py:56
  238.3 1.2 fusion.59
  239.5 0.2 convert_reduce_fusion.1
  239.7 0.2 copy.10
  239.9 0.2 select_reduce_fusion.1
  240.2 0.2 compare_reduce_fusion.1
  240.4 4.6 fusion.21
  245.1 8.2 %convolution_convert_fusion.6 = bf16[1024,1024]{1,0:T(8,128)(2,1)} fusion(bf16[128,4096]{1,0:T(8,128)(2,1)S(1)} %fusion.21, s32[1024]{0:T(1024)S(1)} %select_reduce_fusion.1, pred[1024]{0:T(1024)(128)(4,1)S(1)} %compare_reduce_fusion.1, bf16[1,1024,4096]{2,1,0:T(8,128)(2,1)} %param.11), kind=kOutput, calls=%fused_computation.41 | convolution fusion | flops 1343619072 | bytes 11539456 | tf_op jit(solution)/shard_map/dot_general | solution.py:28
  253.2 0.0 copy-start
  253.2 0.0 reduce-scatter.3.cloned.1.call-update
  253.3 0.0 all-to-all-done
  253.3 1.5 all_to_all.18
  254.8 6.3 %convolution_convert_fusion.10 = bf16[128,1024]{1,0:T(8,128)(2,1)S(1)} fusion(bf16[128,4096]{1,0:T(8,128)(2,1)S(1)} %all_to_all.18, bf16[1,1024,4096]{2,1,0:T(8,128)(2,1)} %param.11), kind=kOutput, calls=%fused_computation.45 | convolution fusion | flops 1073872896 | bytes 9699328 | tf_op jit(solution)/shard_map/dot_general | solution.py:18
  261.1 0.8 all_to_all.19
  261.9 14.0 %all-to-all-start.1 = ((bf16[64,2,1024]{2,1,0:T(2,128)(2,1)}), bf16[64,2,1024]{2,1,0:T(2,128)(2,1)S(1)}, u32[]{:S(2)}, u32[]{:S(2)}) async-start(bf16[64,2,1024]{2,1,0:T(2,128)(2,1)} %all_to_all.19), calls=%async_computation.2 | async-start | bytes 524288 | tf_op jit(solution)/shard_map/all_to_all | solution.py:83
  275.9 0.6 convert_reduce_fusion.4
  277.2 156.3 %pmax.7 = s32[]{:T(128)} all-reduce(s32[]{:T(128)S(6)} %select_n.93), channel_id=1, replica_groups=mesh['section'=16,'expert'=64] {'section','expert'}, use_global_device_ids=true, to_apply=%region_6.7 | all-reduce | flops 1 | bytes 8 | tf_op jit(solution)/shard_map/pmax | solution.py:75
  433.5 0.0 all-to-all-done.1
  433.5 0.1 all_to_all.21
  433.6 35.7 %reduce-scatter.3.cloned.1.call-done = bf16[16,1024]{1,0:T(8,128)(2,1)} async-done(((bf16[1024,1024]{1,0:T(8,128)(2,1)}), bf16[16,1024]{1,0:T(8,128)(2,1)}) %reduce-scatter.3.cloned.1.call-update) | async-done | bytes 32784 | tf_op jit(solution)/shard_map/reduce_scatter | solution.py:64
  469.3 1.0 convolution_convert_fusion.7
  470.4 0.3 fusion.25
  470.6 0.0 copy-done
  470.6 0.0 copy-start.1
  470.7 0.9 while.12
  471.5 2.2 collective-permute-start.1
  473.8 9.3 %collective-permute-done.1 = bf16[128,1024]{1,0:T(8,128)(2,1)S(1)} collective-permute-done((bf16[128,1024]{1,0:T(8,128)(2,1)S(1)}, bf16[128,1024]{1,0:T(8,128)(2,1)S(1)}, u32[]{:S(2)}, u32[]{:S(2)}) %collective-permute-start.1) | collective-permute-done | bytes 262176 | tf_op jit(solution)/shard_map/ppermute | solution.py:13
  483.1 0.0 copy-done.1
  483.1 1.6 fusion.31
  484.7 0.8 pad_maximum_fusion.1
  (5 shorter events, 0.0 us)
Async XLA Ops:
  7.2 231.1 %all-gather.3.cloned.1.call-start = ((), (), s32[]{:S(2)}) async-start(), calls=%async_computation.4 | async-start | bytes 8785920 | tf_op jit(solution)/shard_map/all_gather | solution.py:56
  7.2 16.1 %collective-permute-start = (s32[128]{0:T(128)}, s32[128]{0:T(128)S(1)}, u32[]{:S(2)}, u32[]{:S(2)}) collective-permute-start(s32[128]{0:T(128)} %bitcast.32), channel_id=1, source_target_pairs={{960,0},{0,64},{64,128},{128,192},{192,256},{256,320},{320,384},{3... | collective-permute-start | bytes 1544 | tf_op jit(solution)/shard_map/ppermute | solution.py:13
  29.2 224.1 %all-to-all-start = ((bf16[64,2,4096]{2,1,0:T(2,128)(2,1)}), bf16[64,2,4096]{2,1,0:T(2,128)(2,1)}, u32[]{:S(2)}, u32[]{:S(2)}) async-start(bf16[64,2,4096]{2,1,0:T(2,128)(2,1)} %all_to_all.16), calls=%async_computation.1 | async-start | bytes 2097152 | tf_op jit(solution)/shard_map/all_to_all | solution.py:81
  48.3 421.0 %reduce-scatter.3.cloned.1.call-start = ((), (), s32[]{:S(2)}) async-start(), calls=%async_computation.5 | async-start | bytes 2129920 | tf_op jit(solution)/shard_map/reduce_scatter | solution.py:64
  253.2 217.4 %copy-start = (bf16[128,4096]{1,0:T(8,128)(2,1)S(1)}, bf16[128,4096]{1,0:T(8,128)(2,1)}, u32[]{:S(2)}) copy-start(bf16[128,4096]{1,0:T(8,128)(2,1)} %param.7) | copy-start | bytes 3145732
  261.9 171.6 %all-to-all-start.1 = ((bf16[64,2,1024]{2,1,0:T(2,128)(2,1)}), bf16[64,2,1024]{2,1,0:T(2,128)(2,1)S(1)}, u32[]{:S(2)}, u32[]{:S(2)}) async-start(bf16[64,2,1024]{2,1,0:T(2,128)(2,1)} %all_to_all.19), calls=%async_computation.2 | async-start | bytes 524288 | tf_op jit(solution)/shard_map/all_to_all | solution.py:83
  470.6 12.5 %copy-start.1 = (bf16[128,2048]{1,0:T(8,128)(2,1)S(1)}, bf16[128,2048]{1,0:T(8,128)(2,1)}, u32[]{:S(2)}) copy-start(bf16[128,2048]{1,0:T(8,128)(2,1)} %param.10) | copy-start | bytes 1572868
  471.5 11.6 %collective-permute-start.1 = (bf16[128,1024]{1,0:T(8,128)(2,1)S(1)}, bf16[128,1024]{1,0:T(8,128)(2,1)S(1)}, u32[]{:S(2)}, u32[]{:S(2)}) collective-permute-start(bf16[128,1024]{1,0:T(8,128)(2,1)S(1)} %get-tuple-element.94), channel_id=1, source_target_pairs={{64,0},{128,64},{192,128},{256,192},{320,256},{384,320},{448,384},... | collective-permute-start | bytes 786440 | tf_op jit(solution)/shard_map/ppermute | solution.py:13
Sparse Core Ops, SparseCore 0:
  26.1 212.1 all-gather.2
  253.4 215.8 reduce-scatter.2
